TPU v7x, 512 devices: a whole 4x4x16 slice. The times are simulated.
512 devices in a mesh: tm: 16 (over z), expert: 32 (over x, y, core).
Axes of the slice: x: 4, y: 4, z: 16, core: 2. Of those that a mesh axis runs over, the one named last changes fastest.
Arguments:
- x_in: float32 [32, 4096, 1024], P('expert', 'tm'), may hold values from -6 to 6
- z_gate: bfloat16 [32, 4096, 1024], P('expert', 'tm'), may hold values from -6 to 6
- b_proj: float32 [32, 4096, 128], P('expert', 'tm'), may hold values from -1.5 to 1.5
- c_proj: float32 [32, 4096, 128], P('expert', 'tm'), may hold values from -1.5 to 1.5
- decay_log: float32 [32, 4096, 16], P('expert', 'tm'), as said below
- skip_gain: float32 [16], replicated, may hold values from 0.5 to 2
- residual: float32 [32, 4096, 1024], P('expert', 'tm'), may hold values from -6 to 6
- ssd_gain: float32 [1024], replicated, may hold values from 0.5 to 1.5
- moe_gain: float32 [1024], replicated, may hold values from 0.5 to 1.5
- w_gate: bfloat16 [32, 1024, 1536], P('expert', 'tm'), may hold values from -0.1875 to 0.1875
- w_up: bfloat16 [32, 1024, 1536], P('expert', 'tm'), may hold values from -0.1875 to 0.1875
- w_down: bfloat16 [32, 1536, 1024], P('expert', 'tm'), may hold values from -0.15625 to 0.15625
- routes: int32 [32, 4096, 2], P('expert', 'tm'), may hold values from 0 to 31, all different within a row; in each aligned block of 256 rows (0 to 255, 256 to 511, ..., all dimensions but the last counted through in order) at most 24 rows name the same one
- route_weights: float32 [32, 4096, 2], P('expert', 'tm'), may hold values from 0.2 to 1
Outputs:
- mixed: float32 [32, 4096, 1024], P('expert', 'tm')
Inputs may be any that keep to these rules, and one draw needn't show every extreme that they name: `routes`: the two experts of a time step differ. Among the time steps of one device no expert is named more than 24 times, and in every draw some device names some expert exactly 24 times. `decay_log`: every entry is at most zero.
All inputs are finite; a program needn't handle non-finite values.
Results may differ from a plain program's by a relative error of at most 0.0021.
Values may be sent and summed in bfloat16 or wider, within the bound.
No kernel may reach another device: no remote copies, remote signals or barrier semaphores. Data moves between devices by JAX's collectives and lax.ppermute only.
A program may use at most 64 MiB of HBM per device.

v0:
```python
import math
import jax
import jax.numpy as jnp
from jax import lax
from jax.sharding import PartitionSpec as P

exact_mode = lax.Precision.HIGHEST


def carried_in_2(value, axis, join, neutral):
    count, mine = (lax.axis_size(axis), lax.axis_index(axis))
    pieces = jax.tree.map(lambda part: lax.all_gather(part, axis), value)
    running = jax.tree.map(
        lambda part, zero: jnp.full_like(part, 0) + jnp.asarray(zero, part.dtype), value, neutral
    )

    def lap(position, running):
        longer = join(running, jax.tree.map(lambda part: part[position], pieces))
        return jax.tree.map(lambda new, old: jnp.where(position < mine, new, old), longer, running)

    return lax.fori_loop(0, count - 1, lap, running)


def group_carry(state, values, b_rows, running):
    remains = jnp.exp(running[-1][None, :] - running)
    fresh = jnp.einsum("jhp,jn->hpn", values * remains[:, :, None], b_rows, precision=exact_mode)
    return jnp.exp(running[-1])[:, None, None] * state + fresh


def group_step(state, inputs, skip_gain):
    values, b_rows, c_rows, log_rates = inputs
    length = values.shape[0]
    running = jnp.cumsum(log_rates, axis=0)
    across = running.T[:, :, None] - running.T[:, None, :]
    places = jnp.arange(length)
    causal = (places[:, None] >= places[None, :])[None]
    masked = jnp.where(causal, jnp.exp(jnp.where(causal, across, 0.0)), 0.0)
    scores = jnp.dot(c_rows, b_rows.T, precision=exact_mode)
    mixing = masked * scores[None]
    output = jnp.einsum("hij,jhp->ihp", mixing, values, precision=exact_mode)
    output = output + jnp.exp(running)[:, :, None] * jnp.einsum(
        "in,hpn->ihp", c_rows, state, precision=exact_mode
    )
    output = output + skip_gain[None, :, None] * values
    return (group_carry(state, values, b_rows, running), output)


def incoming_state(through, local_end):

    def combine(earlier, later):
        return (earlier[0] * later[0], later[0][:, None, None] * earlier[1] + later[1])

    prefix = carried_in_2(
        (through, local_end), "tm", combine, (jnp.ones_like(through), jnp.zeros_like(local_end))
    )
    return prefix[1]


def rms_scale(rows, gain):
    return gain * rows / jnp.sqrt(jnp.mean(rows * rows, axis=-1, keepdims=True) + 1e-05)


def per_device(
    x_in,
    z_gate,
    b_proj,
    c_proj,
    decay_log,
    skip_gain,
    residual,
    ssd_gain,
    moe_gain,
    w_gate,
    w_up,
    w_down,
    routes,
    route_weights,
):
    heads = skip_gain.shape[0]
    model_width = x_in.shape[2]
    width = model_width // heads
    length = x_in.shape[1]
    block = math.gcd(length, 256)
    count = length // block
    values = x_in[0].reshape(length, heads, width)
    b_rows = b_proj[0]
    c_rows = c_proj[0]
    log_rates = decay_log[0]
    inputs = (
        values.reshape(count, block, heads, width),
        b_rows.reshape(count, block, -1),
        c_rows.reshape(count, block, -1),
        log_rates.reshape(count, block, heads),
    )
    start = jnp.zeros((heads, width, b_rows.shape[1]), jnp.float32)
    through = jnp.exp(jnp.sum(log_rates, axis=0))
    local_end, outputs = lax.scan(
        lambda state, piece: group_step(state, piece, skip_gain), start, inputs
    )
    incoming = incoming_state(through, local_end)
    running = jnp.cumsum(log_rates, axis=0)
    carried_in = jnp.exp(running)[:, :, None] * jnp.einsum(
        "in,hpn->ihp", c_rows, incoming, precision=exact_mode
    )
    mixed_ssd = (outputs.reshape(length, heads, width) + carried_in).reshape(length, model_width)
    gated = mixed_ssd * jax.nn.silu(z_gate[0].astype(jnp.float32))
    hres = residual[0] + rms_scale(gated, ssd_gain)
    normed = rms_scale(hres, moe_gain).astype(jnp.bfloat16)
    expert_count = lax.axis_size("expert")
    capacity = max(2, 3 * length // expert_count)
    flat_routes = routes[0].reshape(-1)
    picked_one = (flat_routes[:, None] == jnp.arange(expert_count)[None, :]).astype(jnp.int32)
    earlier_hits = jnp.cumsum(picked_one, axis=0) - picked_one
    slot_index = jnp.sum(earlier_hits * picked_one, axis=1)
    target = flat_routes * capacity + slot_index
    repeated = jnp.broadcast_to(normed[:, None, :], (length, 2, model_width)).reshape(
        2 * length, model_width
    )
    outgoing = (
        jnp.zeros((expert_count * capacity, model_width), jnp.bfloat16).at[target].set(repeated)
    )
    received = lax.all_to_all(
        outgoing.reshape(expert_count, capacity, model_width),
        "expert",
        split_axis=0,
        concat_axis=0,
        tiled=True,
    )
    received = received.reshape(expert_count * capacity, model_width)
    slot_rows = expert_count * capacity
    columns = received
    gate = jnp.dot(
        columns,
        lax.all_gather(w_gate[0], "tm", axis=0, tiled=True),
        preferred_element_type=jnp.float32,
    )
    upper = jnp.dot(
        columns,
        lax.all_gather(w_up[0], "tm", axis=0, tiled=True),
        preferred_element_type=jnp.float32,
    )
    hidden = (jax.nn.silu(gate) * upper).astype(jnp.bfloat16)
    columns = hidden
    produced = jnp.dot(
        columns,
        lax.all_gather(w_down[0], "tm", axis=0, tiled=True),
        preferred_element_type=jnp.float32,
    ).astype(jnp.bfloat16)
    back = lax.all_to_all(
        produced.reshape(expert_count, capacity, model_width),
        "expert",
        split_axis=0,
        concat_axis=0,
        tiled=True,
    )
    back = back.reshape(slot_rows, model_width)
    fetched = back[target].astype(jnp.float32).reshape(length, 2, model_width)
    weights_here = route_weights[0]
    moe = fetched[:, 0, :] * weights_here[:, 0:1] + fetched[:, 1, :] * weights_here[:, 1:2]
    return (hres + moe).reshape(1, length, model_width)


def solution(mesh):
    in_specs = (
        P("expert", "tm", None),
        P("expert", "tm", None),
        P("expert", "tm", None),
        P("expert", "tm", None),
        P("expert", "tm", None),
        P(),
        P("expert", "tm", None),
        P(),
        P(),
        P("expert", "tm", None),
        P("expert", "tm", None),
        P("expert", "tm", None),
        P("expert", "tm", None),
        P("expert", "tm", None),
    )
    out_specs = P("expert", "tm", None)
    return jax.shard_map(
        per_device, mesh=mesh, in_specs=in_specs, out_specs=out_specs, check_vma=False
    )
```

profile of v0, /device:TPU:1, one launch (start us, length us, event | category | flops | bytes accessed | tf_op | source)
XLA Modules:
  0.0 405.9 jit_solution(9429766804105325587)
XLA Ops:
  8.5 1.6 copy.54
  10.2 1.8 convolution_add_fusion
  15.0 1.3 dynamic-slice
  17.1 32.2 %all-reduce = f32[256]{0:T(256)S(1)} all-reduce(f32[256]{0:T(256)S(1)} %exponential_dynamic-update-slice_fusion), channel_id=2, replica_groups=mesh['tm'=16,'expert'=32] {'tm'}, use_global_device_ids=true, to_apply=%add | all-reduce | flops 256 | bytes 2048
  49.4 1.2 copy.57
  52.4 5.1 %fusion.24 = f32[256,16,64]{0,2,1:T(8,128)S(1)} fusion(f32[256,16,64]{0,2,1:T(8,128)S(1)} %bitcast.161, f32[256,256]{1,0:T(8,128)S(1)} %fusion.49, f32[16,256]{1,0:T(8,128)S(1)} %get-tuple-element.159, pred[256,256]{1,0:T(8,128)(4,1)S(1)} %iota_compare_fusion), kind=kOutput, calls=%fused_computation.23 | convolution fusion | flops 809500672 | bytes 2441216 | tf_op jit(solution)/shard_map/while/body/eval_jaxpr/hij,jhp->ihp/dot_general | solution.py:40
  57.6 2.1 fusion.31
  59.7 64.1 %all-gather.10.cloned.1.call-done = f32[256,64,128]{2,1,0:T(8,128)} async-done(((f32[16,64,128]{2,1,0:T(8,128)}), f32[256,64,128]{2,1,0:T(8,128)}) %all-gather.10.cloned.1.call-update) | async-done | bytes 8388624 | tf_op jit(solution)/shard_map/all_gather | solution.py:12
  123.7 18.2 %while.9 = (s32[]{:T(128)}, f32[16,64,128]{2,1,0:T(8,128)S(1)}, s32[]{:T(128)}, f32[16,16]{1,0:T(8,128)S(1)}, f32[16,16,64,128]{3,2,1,0:T(8,128)}, /*index=5*/s32[]{:T(128)}, s32[]{:T(128)}) while((s32[]{:T(128)}, f32[16,64,128]{2,1,0:T(8,128)S(1)}, s32[]{:T(128)}, f32[16,16]{1,0:T(8,128)S(1)}, f32[16,16,64,128]{3,2,1,0:T(8,128)}, ...), condition=%wide.region_4.5_spmd.clone, body=%wide.region_3.4_spmd.clone.sunk | while | flops 524292 | bytes 1573161 | solution.py:21
  125.0 1.2 fusion.70
  126.2 1.2 fusion.70
  129.8 1.2 fusion.70
  131.0 1.2 fusion.70
  139.5 1.2 fusion.70
  142.0 2.8 multiply_reduce_fusion.1
  144.8 1.3 copy.62
  146.1 1.8 multiply_reduce_fusion
  148.7 1.2 reshape.351
  149.9 4.5 %scatter_custom_fusion = bf16[768,1024]{1,0:T(8,128)(2,1)} fusion(s32[512]{0:T(512)S(1)} %bitcast.171, bf16[512,1024]{1,0:T(8,128)(2,1)} %reshape.351, bf16[]{:T(256)} %constant.72.clone.1), kind=kCustom, calls=%fused_computation.51 | custom fusion | bytes 1573376 | tf_op jit(solution)/shard_map/scatter | solution.py:120
  154.4 7.5 %all-to-all-start = ((bf16[32,24,1024]{2,1,0:T(8,128)(2,1)}), bf16[32,24,1024]{2,1,0:T(8,128)(2,1)S(1)}, u32[]{:S(2)}, u32[]{:S(2)}) async-start(bf16[32,24,1024]{2,1,0:T(8,128)(2,1)} %bitcast.23), calls=%async_computation | async-start | bytes 3145728 | tf_op jit(solution)/shard_map/all_to_all | solution.py:122
  162.0 29.4 %all-gather.12.cloned.1.call-done = bf16[1,1024,1536]{2,1,0:T(8,128)(2,1)} async-done(((bf16[1,64,1536]{2,1,0:T(8,128)(2,1)}), bf16[1,1024,1536]{2,1,0:T(8,128)(2,1)}) %all-gather.12.cloned.1.call-update) | async-done | bytes 3145744 | tf_op jit(solution)/shard_map/all_gather | solution.py:134
  191.3 6.1 %fusion.10 = f32[768,1536]{1,0:T(8,128)} fusion(bf16[768,1024]{1,0:T(8,128)(2,1)S(1)} %bitcast.166, bf16[1,1024,1536]{2,1,0:T(8,128)(2,1)} %all-gather.12.cloned.1.call-done), kind=kOutput, calls=%fused_computation.15 | convolution fusion | flops 2415919104 | bytes 9437184 | tf_op jit(solution)/shard_map/dot_general | solution.py:132
  197.4 69.0 %all-gather.14.cloned.1.call-done = bf16[1,1024,1536]{2,1,0:T(8,128)(2,1)} async-done(((bf16[1,64,1536]{2,1,0:T(8,128)(2,1)}), bf16[1,1024,1536]{2,1,0:T(8,128)(2,1)}) %all-gather.14.cloned.1.call-update) | async-done | bytes 3145744 | tf_op jit(solution)/shard_map/all_gather | solution.py:139
  266.4 75.2 %all-gather.16.cloned.1.call-done = bf16[1,1536,1024]{2,1,0:T(8,128)(2,1)} async-done(((bf16[1,96,1024]{2,1,0:T(8,128)(2,1)}), bf16[1,1536,1024]{2,1,0:T(8,128)(2,1)}) %all-gather.16.cloned.1.call-update) | async-done | bytes 3145744 | tf_op jit(solution)/shard_map/all_gather | solution.py:146
  341.6 10.5 %fusion.19 = bf16[768,1024]{1,0:T(8,128)(2,1)} fusion(bf16[1,1536,1024]{2,1,0:T(8,128)(2,1)} %all-gather.16.cloned.1.call-done, f32[768,1536]{1,0:T(8,128)} %fusion.10, bf16[768,1024]{1,0:T(8,128)(2,1)S(1)} %bitcast.167, bf16[1,1024,1536]{2,1,0:T(8,128)(2,1)} %all-gather.14.cloned.1.call-done), kind=kOutput, calls=%fused_computation.22 | convolution fusion | flops 4839702528 | bytes 14155776 | tf_op jit(solution)/shard_map/dot_general | solution.py:144
  352.0 16.2 %all-to-all-start.1 = ((bf16[32,24,1024]{2,1,0:T(8,128)(2,1)}), bf16[32,24,1024]{2,1,0:T(8,128)(2,1)S(1)}, u32[]{:S(2)}, u32[]{:S(2)}) async-start(bf16[32,24,1024]{2,1,0:T(8,128)(2,1)} %bitcast.168), calls=%async_computation.1 | async-start | bytes 3145728 | tf_op jit(solution)/shard_map/all_to_all | solution.py:149
  368.3 1.3 copy.56
  369.6 21.3 %all-to-all-done.1 = bf16[32,24,1024]{2,1,0:T(8,128)(2,1)S(1)} async-done(((bf16[32,24,1024]{2,1,0:T(8,128)(2,1)}), bf16[32,24,1024]{2,1,0:T(8,128)(2,1)S(1)}, u32[]{:S(2)}, u32[]{:S(2)}) %all-to-all-start.1) | async-done | bytes 1572896 | tf_op jit(solution)/shard_map/all_to_all | solution.py:149
  390.9 2.8 gather_fusion
  393.7 2.4 reshape.338
  396.1 1.6 fusion.61
  397.7 1.6 fusion.34
  (94 shorter events, 19.6 us)
Async XLA Ops:
  6.5 8.1 %copy-start = (f32[1,256,128]{2,1,0:T(8,128)S(1)}, f32[1,256,128]{2,1,0:T(8,128)}, u32[]{:S(2)}) copy-start(f32[1,256,128]{2,1,0:T(8,128)} %param.19) | copy-start | bytes 393220
  6.5 3.6 copy-start.5
  6.5 117.2 %all-gather.10.cloned.1.call-start = ((), (), s32[]{:S(2)}) async-start(), calls=%async_computation.2 | async-start | bytes 8912896 | tf_op jit(solution)/shard_map/all_gather | solution.py:12
  8.4 5.6 %copy-start.6 = (f32[1,256,16]{1,2,0:T(8,128)S(1)}, f32[1,256,16]{1,2,0:T(8,128)}, u32[]{:S(2)}) copy-start(f32[1,256,16]{1,2,0:T(8,128)} %param.20) | copy-start | bytes 49156
  8.5 5.7 %copy-start.8 = (s32[1,256,2]{1,2,0:T(2,128)S(1)}, s32[1,256,2]{1,2,0:T(2,128)}, u32[]{:S(2)}) copy-start(s32[1,256,2]{1,2,0:T(2,128)} %param.28) | copy-start | bytes 6148
  10.0 39.4 %copy-start.1 = (bf16[1,256,1024]{2,1,0:T(8,128)(2,1)S(1)}, bf16[1,256,1024]{2,1,0:T(8,128)(2,1)}, u32[]{:S(2)}) copy-start(bf16[1,256,1024]{2,1,0:T(8,128)(2,1)} %param.17) | copy-start | bytes 1572868
  12.0 179.4 %all-gather.12.cloned.1.call-start = ((), (), s32[]{:S(2)}) async-start(), calls=%async_computation.3 | async-start | bytes 3342336 | tf_op jit(solution)/shard_map/all_gather | solution.py:134
  12.7 253.7 %all-gather.14.cloned.1.call-start = ((), (), s32[]{:S(2)}) async-start(), calls=%async_computation.4 | async-start | bytes 3342336 | tf_op jit(solution)/shard_map/all_gather | solution.py:139
  13.4 328.1 %all-gather.16.cloned.1.call-start = ((), (), s32[]{:S(2)}) async-start(), calls=%async_computation.5 | async-start | bytes 3342336 | tf_op jit(solution)/shard_map/all_gather | solution.py:146
  52.4 5.1 %copy-start.11 = (f32[16]{0:T(128)S(1)}, f32[16]{0:T(128)}, u32[]{:S(2)}) copy-start(f32[16]{0:T(128)} %param.21) | copy-start | bytes 196
  142.0 4.2 %copy-start.3 = (f32[1,256,1024]{2,1,0:T(8,128)S(1)}, f32[1,256,1024]{2,1,0:T(8,128)}, u32[]{:S(2)}) copy-start(f32[1,256,1024]{2,1,0:T(8,128)} %param.22) | copy-start | bytes 3145732
  142.0 4.1 %copy-start.7 = (f32[1024]{0:T(1024)S(1)}, f32[1024]{0:T(1024)}, u32[]{:S(2)}) copy-start(f32[1024]{0:T(1024)} %param.23) | copy-start | bytes 12292
  144.8 3.1 copy-start.9
  154.4 36.9 %all-to-all-start = ((bf16[32,24,1024]{2,1,0:T(8,128)(2,1)}), bf16[32,24,1024]{2,1,0:T(8,128)(2,1)S(1)}, u32[]{:S(2)}, u32[]{:S(2)}) async-start(bf16[32,24,1024]{2,1,0:T(8,128)(2,1)} %bitcast.23), calls=%async_computation | async-start | bytes 3145728 | tf_op jit(solution)/shard_map/all_to_all | solution.py:122
  352.0 16.2 %copy-start.10 = (f32[1,256,2]{1,2,0:T(2,128)S(1)}, f32[1,256,2]{1,2,0:T(2,128)}, u32[]{:S(2)}) copy-start(f32[1,256,2]{1,2,0:T(2,128)} %param.29) | copy-start | bytes 6148
  352.0 38.9 %all-to-all-start.1 = ((bf16[32,24,1024]{2,1,0:T(8,128)(2,1)}), bf16[32,24,1024]{2,1,0:T(8,128)(2,1)S(1)}, u32[]{:S(2)}, u32[]{:S(2)}) async-start(bf16[32,24,1024]{2,1,0:T(8,128)(2,1)} %bitcast.168), calls=%async_computation.1 | async-start | bytes 3145728 | tf_op jit(solution)/shard_map/all_to_all | solution.py:149
  396.1 1.7 copy-start.2
  396.1 1.7 copy-start.4
Sparse Core Ops, SparseCore 0:
  12.1 111.6 all-gather.9
  125.8 65.4 all-gather.11
  193.4 72.9 all-gather.13
  268.3 73.2 all-gather.15
where the time goes:
time: 407 us; the launch traced here: 406 us
  waiting for transfers between devices  261 us (64%)
  blocking collectives  32.2 us (8%)
  matrix products  28.7 us (7%)
  starting transfers between devices  23.9 us (6%)
  other arithmetic  23.6 us (6%)
  local copies, waits for them, and re-layouts  22.1 us (5%)
  between operations  14.1 us (3%)
    all_gather x1, waiting for transfers between devices, per_device(): lax.all_gather(w_down[0], 'tm', axis=0, tiled=True)  75.2 us
    all_gather x1, waiting for transfers between devices, per_device(): lax.all_gather(w_up[0], 'tm', axis=0, tiled=True)  69 us
    all_gather x1, waiting for transfers between devices, carried_in_2(): pieces = jax.tree.map(lambda part: lax.all_gather(part, axis), value)  64.1 us
    unnamed x1, blocking collectives  32.2 us
    all_gather x1, waiting for transfers between devices, per_device(): lax.all_gather(w_gate[0], 'tm', axis=0, tiled=True)  29.4 us
    all_to_all x1, waiting for transfers between devices, per_device(): lax.all_to_all(produced.reshape(expert_count, capacity, model_width), 'ex...  21.3 us
    select_n x15, other arithmetic, lap(): jnp.where(position < mine, new, old)  17.6 us
    all_to_all x1, starting transfers between devices, per_device(): lax.all_to_all(produced.reshape(expert_count, capacity, model_width), 'ex...  16.2 us
  transfers between devices with their start and end apart: 6, of which 5 were waited for; matrix products, arithmetic and copies ran while one was open for 12% of the time, Pallas kernels for 0%

commit v1 on v0

--- a/solution.py
+++ b/solution.py
@@ -131,7 +131,9 @@
     columns = received
     gate = jnp.dot(
         columns,
-        lax.all_gather(w_gate[0], "tm", axis=0, tiled=True),
+        jnp.concatenate(
+            lax.all_to_all(jnp.stack([w_gate[0]] * lax.axis_size("tm")), "tm", 0, 0), axis=0
+        ),
         preferred_element_type=jnp.float32,
     )
     upper = jnp.dot(

time: 407 us -> 465 us (1.14)
  blocking collectives: 32.2 us -> 217 us
  waiting for transfers between devices: 261 us -> 123 us
  starting transfers between devices: 23.9 us -> 32.2 us
    unnamed x1, blocking collectives: 32.2 us -> 186 us
    all_gather x1, waiting for transfers between devices: 69 us -> 0.71 us  [per_device(): lax.all_gather(w_up[0], 'tm', axis=0, tiled=True)]
    all_gather x1, waiting for transfers between devices: 64.1 us -> 24.2 us  [carried_in_2(): pieces = jax.tree.map(lambda part: lax.all_gather(part, axis), value)]
    all_to_all x0 -> x1, blocking collectives: none -> 30.2 us  [per_device(): lax.all_to_all(outgoing.reshape(expert_count, capacity, model_width), 'ex...]
    all_gather x1 -> x0, waiting for transfers between devices: 29.4 us -> none  [per_device(): lax.all_gather(w_gate[0], 'tm', axis=0, tiled=True)]
    all_to_all x1, starting transfers between devices: 7.54 us -> 15.9 us  [per_device(): lax.all_to_all(jnp.stack([w_gate[0]] * lax.axis_size('tm')), 'tm', 0, 0)]
  transfers between devices with their start and end apart: 6 -> 5, of which waited for: 5 -> 4; matrix products, arithmetic and copies ran while one was open for 12% -> 11% of each run, Pallas kernels for 0% -> 0%
where the time goes in v1:
time: 465 us; the launch traced here: 463 us
  blocking collectives  217 us (47%)
  waiting for transfers between devices  123 us (26%)
  starting transfers between devices  32.2 us (7%)
  matrix products  29.1 us (6%)
  local copies, waits for them, and re-layouts  24.6 us (5%)
  other arithmetic  23.5 us (5%)
  between operations  14.1 us (3%)
    unnamed x1, blocking collectives  186 us
    all_gather x1, waiting for transfers between devices, per_device(): lax.all_gather(w_down[0], 'tm', axis=0, tiled=True)  75.1 us
    all_to_all x1, blocking collectives, per_device(): lax.all_to_all(outgoing.reshape(expert_count, capacity, model_width), 'ex...  30.2 us
    all_gather x1, waiting for transfers between devices, carried_in_2(): pieces = jax.tree.map(lambda part: lax.all_gather(part, axis), value)  24.2 us
    all_to_all x1, waiting for transfers between devices, per_device(): lax.all_to_all(produced.reshape(expert_count, capacity, model_width), 'ex...  21.3 us
    select_n x15, other arithmetic, lap(): jnp.where(position < mine, new, old)  17.6 us
    all_to_all x1, starting transfers between devices, per_device(): lax.all_to_all(produced.reshape(expert_count, capacity, model_width), 'ex...  16.2 us
    all_to_all x1, starting transfers between devices, per_device(): lax.all_to_all(jnp.stack([w_gate[0]] * lax.axis_size('tm')), 'tm', 0, 0)  15.9 us
  transfers between devices with their start and end apart: 5, of which 4 were waited for; matrix products, arithmetic and copies ran while one was open for 11% of the time, Pallas kernels for 0%

profile of v1, /device:TPU:1, one launch (start us, length us, event | category | flops | bytes accessed | tf_op | source)
XLA Modules:
  0.0 463.4 jit_solution(15332401351944107014)
XLA Ops:
  8.5 1.6 copy.54
  10.2 1.8 convolution_add_fusion
  12.7 1.9 stack.3
  14.7 15.9 %all-to-all-start.1 = ((bf16[16,64,1536]{2,1,0:T(8,128)(2,1)}), bf16[16,64,1536]{2,1,0:T(8,128)(2,1)}, u32[]{:S(2)}, u32[]{:S(2)}) async-start(bf16[16,64,1536]{2,1,0:T(8,128)(2,1)} %stack.3), calls=%async_computation.1 | async-start | bytes 6291456 | tf_op jit(solution)/shard_map/all_to_all | solution.py:135
  31.9 1.3 dynamic-slice
  34.0 186.5 %all-reduce = f32[256]{0:T(256)S(1)} all-reduce(f32[256]{0:T(256)S(1)} %exponential_dynamic-update-slice_fusion), channel_id=2, replica_groups=mesh['tm'=16,'expert'=32] {'tm'}, use_global_device_ids=true, to_apply=%add | all-reduce | flops 256 | bytes 2048
  220.5 1.2 copy.57
  224.0 5.1 %fusion.22 = f32[256,16,64]{0,2,1:T(8,128)S(1)} fusion(f32[256,16,64]{0,2,1:T(8,128)S(1)} %bitcast.161, f32[256,256]{1,0:T(8,128)S(1)} %fusion.47, f32[16,256]{1,0:T(8,128)S(1)} %get-tuple-element.159, pred[256,256]{1,0:T(8,128)(4,1)S(1)} %iota_compare_fusion), kind=kOutput, calls=%fused_computation.21 | convolution fusion | flops 809500672 | bytes 2441216 | tf_op jit(solution)/shard_map/while/body/eval_jaxpr/hij,jhp->ihp/dot_general | solution.py:40
  229.1 2.0 fusion.29
  231.2 24.2 %all-gather.8.cloned.1.call-done = f32[256,64,128]{2,1,0:T(8,128)} async-done(((f32[16,64,128]{2,1,0:T(8,128)}), f32[256,64,128]{2,1,0:T(8,128)}) %all-gather.8.cloned.1.call-update) | async-done | bytes 8388624 | tf_op jit(solution)/shard_map/all_gather | solution.py:12
  255.4 18.2 %while.9 = (s32[]{:T(128)}, f32[16,64,128]{2,1,0:T(8,128)S(1)}, s32[]{:T(128)}, f32[16,16]{1,0:T(8,128)S(1)}, f32[16,16,64,128]{3,2,1,0:T(8,128)}, /*index=5*/s32[]{:T(128)}, s32[]{:T(128)}) while((s32[]{:T(128)}, f32[16,64,128]{2,1,0:T(8,128)S(1)}, s32[]{:T(128)}, f32[16,16]{1,0:T(8,128)S(1)}, f32[16,16,64,128]{3,2,1,0:T(8,128)}, ...), condition=%wide.region_4.5_spmd.clone, body=%wide.region_3.4_spmd.clone.sunk | while | flops 524292 | bytes 1573161 | solution.py:21
  257.8 1.2 fusion.70
  259.0 1.2 fusion.70
  260.2 1.2 fusion.70
  263.9 1.2 fusion.70
  265.1 1.2 fusion.70
  273.6 2.8 multiply_reduce_fusion.1
  276.4 1.3 copy.62
  277.7 1.8 multiply_reduce_fusion
  280.2 1.2 reshape.356
  281.4 3.9 scatter_custom_fusion
  285.4 30.2 %all_to_all.15 = bf16[32,24,1024]{2,1,0:T(8,128)(2,1)S(1)} all-to-all(bf16[32,24,1024]{2,1,0:T(8,128)(2,1)S(1)} %bitcast.163), channel_id=1, replica_groups=mesh['tm'=16,'expert'=32] {'expert'}, dimensions={0} | all-to-all | bytes 3145728 | tf_op jit(solution)/shard_map/all_to_all | solution.py:122
  316.7 6.1 %fusion.61 = f32[768,1536]{1,0:T(8,128)} fusion(bf16[768,1024]{1,0:T(8,128)(2,1)S(1)} %bitcast.168, bf16[1024,1536]{1,0:T(8,128)(2,1)} %bitcast.26), kind=kOutput, calls=%fused_computation.88 | convolution fusion | flops 2415919104 | bytes 9437184 | tf_op jit(solution)/shard_map/dot_general | solution.py:132
  323.5 75.1 %all-gather.12.cloned.1.call-done = bf16[1,1536,1024]{2,1,0:T(8,128)(2,1)} async-done(((bf16[1,96,1024]{2,1,0:T(8,128)(2,1)}), bf16[1,1536,1024]{2,1,0:T(8,128)(2,1)}) %all-gather.12.cloned.1.call-update) | async-done | bytes 3145744 | tf_op jit(solution)/shard_map/all_gather | solution.py:148
  398.6 10.9 %fusion.17 = bf16[768,1024]{1,0:T(8,128)(2,1)} fusion(bf16[1,1536,1024]{2,1,0:T(8,128)(2,1)} %all-gather.12.cloned.1.call-done, f32[768,1536]{1,0:T(8,128)} %fusion.61, bf16[768,1024]{1,0:T(8,128)(2,1)} %bitcast.169, bf16[1,1024,1536]{2,1,0:T(8,128)(2,1)} %all-gather.10.cloned.1.call-done), kind=kOutput, calls=%fused_computation.20 | convolution fusion | flops 4839702528 | bytes 14155776 | tf_op jit(solution)/shard_map/dot_general | solution.py:146
  409.5 16.2 %all-to-all-start.2 = ((bf16[32,24,1024]{2,1,0:T(8,128)(2,1)}), bf16[32,24,1024]{2,1,0:T(8,128)(2,1)S(1)}, u32[]{:S(2)}, u32[]{:S(2)}) async-start(bf16[32,24,1024]{2,1,0:T(8,128)(2,1)} %bitcast.167), calls=%async_computation.2 | async-start | bytes 3145728 | tf_op jit(solution)/shard_map/all_to_all | solution.py:151
  425.7 1.3 copy.56
  427.1 21.3 %all-to-all-done.2 = bf16[32,24,1024]{2,1,0:T(8,128)(2,1)S(1)} async-done(((bf16[32,24,1024]{2,1,0:T(8,128)(2,1)}), bf16[32,24,1024]{2,1,0:T(8,128)(2,1)S(1)}, u32[]{:S(2)}, u32[]{:S(2)}) %all-to-all-start.2) | async-done | bytes 1572896 | tf_op jit(solution)/shard_map/all_to_all | solution.py:151
  448.4 2.8 gather_fusion
  451.2 2.4 reshape.343
  453.6 1.6 fusion.59
  455.2 1.6 fusion.32
  (97 shorter events, 21.0 us)
Async XLA Ops:
  6.5 217.1 %copy-start = (f32[1,256,128]{2,1,0:T(8,128)S(1)}, f32[1,256,128]{2,1,0:T(8,128)}, u32[]{:S(2)}) copy-start(f32[1,256,128]{2,1,0:T(8,128)} %param.19) | copy-start | bytes 393220
  6.5 3.6 copy-start.6
  6.5 248.8 %all-gather.8.cloned.1.call-start = ((), (), s32[]{:S(2)}) async-start(), calls=%async_computation.3 | async-start | bytes 8912896 | tf_op jit(solution)/shard_map/all_gather | solution.py:12
  8.4 4.3 copy-start.7
  12.0 311.5 %all-gather.10.cloned.1.call-start = ((), (), s32[]{:S(2)}) async-start(), calls=%async_computation.4 | async-start | bytes 3342336 | tf_op jit(solution)/shard_map/all_gather | solution.py:141
  14.7 16.7 %copy-start.8 = (f32[1,256,16]{1,2,0:T(8,128)S(1)}, f32[1,256,16]{1,2,0:T(8,128)}, u32[]{:S(2)}) copy-start(f32[1,256,16]{1,2,0:T(8,128)} %param.20) | copy-start | bytes 49156
  14.7 16.8 %copy-start.10 = (s32[1,256,2]{1,2,0:T(2,128)S(1)}, s32[1,256,2]{1,2,0:T(2,128)}, u32[]{:S(2)}) copy-start(s32[1,256,2]{1,2,0:T(2,128)} %param.28) | copy-start | bytes 6148
  14.7 205.9 %copy-start.1 = (bf16[1,256,1024]{2,1,0:T(8,128)(2,1)S(1)}, bf16[1,256,1024]{2,1,0:T(8,128)(2,1)}, u32[]{:S(2)}) copy-start(bf16[1,256,1024]{2,1,0:T(8,128)(2,1)} %param.17) | copy-start | bytes 1572868
  14.7 270.7 %all-to-all-start.1 = ((bf16[16,64,1536]{2,1,0:T(8,128)(2,1)}), bf16[16,64,1536]{2,1,0:T(8,128)(2,1)}, u32[]{:S(2)}, u32[]{:S(2)}) async-start(bf16[16,64,1536]{2,1,0:T(8,128)(2,1)} %stack.3), calls=%async_computation.1 | async-start | bytes 6291456 | tf_op jit(solution)/shard_map/all_to_all | solution.py:135
  30.6 368.0 %all-gather.12.cloned.1.call-start = ((), (), s32[]{:S(2)}) async-start(), calls=%async_computation.5 | async-start | bytes 3342336 | tf_op jit(solution)/shard_map/all_gather | solution.py:148
  224.0 5.1 %copy-start.13 = (f32[16]{0:T(128)S(1)}, f32[16]{0:T(128)}, u32[]{:S(2)}) copy-start(f32[16]{0:T(128)} %param.21) | copy-start | bytes 196
  273.5 4.2 copy-start.3
  273.6 4.1 copy-start.9
  276.4 3.1 copy-start.11
  315.6 1.2 copy-start.5
  409.5 16.2 %copy-start.12 = (f32[1,256,2]{1,2,0:T(2,128)S(1)}, f32[1,256,2]{1,2,0:T(2,128)}, u32[]{:S(2)}) copy-start(f32[1,256,2]{1,2,0:T(2,128)} %param.29) | copy-start | bytes 6148
  409.5 38.9 %all-to-all-start.2 = ((bf16[32,24,1024]{2,1,0:T(8,128)(2,1)}), bf16[32,24,1024]{2,1,0:T(8,128)(2,1)S(1)}, u32[]{:S(2)}, u32[]{:S(2)}) async-start(bf16[32,24,1024]{2,1,0:T(8,128)(2,1)} %bitcast.167), calls=%async_computation.2 | async-start | bytes 3145728 | tf_op jit(solution)/shard_map/all_to_all | solution.py:151
  453.5 1.7 copy-start.2
  453.5 1.7 copy-start.4
Sparse Core Ops, SparseCore 0:
  12.1 243.2 all-gather.7
  257.4 66.0 all-gather.9
  325.6 72.9 all-gather.11
